TPU v7x, 256 devices: a whole 4x4x8 slice. The times are simulated.
256 devices in a mesh: row: 16 (over x, y), col: 16 (over z, core).
Axes of the slice: x: 4, y: 4, z: 8, core: 2. Of those that a mesh axis runs over, the one named last changes fastest.
Arguments:
- start_block: float32 [65536, 128], P(('row', 'col')), may hold values from -6 to 6
- vertex_scale: float32 [65536], P(('row', 'col')), may hold values from 0.015625 to 0.0625
- adj_tiles: bfloat16 [16, 16, 64, 128, 128], P('row', 'col'), may hold values from 0 to 1
- tile_row: int32 [16, 16, 64], P('row', 'col'), may hold values from 0 to 31
- tile_col: int32 [16, 16, 64], P('row', 'col'), may hold values from 0 to 31
- live_count: int32 [16, 16], P('row', 'col'), may hold values from 16 to 64, as said below
- rotation_first: float32 [256, 128], replicated, may hold values from -0.375 to 0.375
- rotation_second: float32 [384, 128], replicated, may hold values from -0.3125 to 0.3125
Outputs:
- final_block: float32 [65536, 128], P(('row', 'col'))
- final_image: float32 [65536, 128], P(('row', 'col'))
Inputs may be any that keep to these rules, and one draw needn't show every extreme that they name: Slots from live_count on are ignored; at least one device has all 64 slots live in every draw.
All inputs are finite; a program needn't handle non-finite values.
Results may differ from a plain program's by a relative error of at most 0.01.
Values may be sent and summed in bfloat16 or wider, within the bound.
A program may use at most 64 MiB of HBM per device.

v0:
```python
import jax
import jax.numpy as jnp
from jax import lax
from jax.sharding import PartitionSpec as P

HIGH = lax.Precision.HIGHEST


def tile_products(tiles_here, cols_here, count_here, flat_panel, span_slots, tile_side, width_k):
    alive_mask = jnp.arange(span_slots, dtype=jnp.int32) < count_here
    pieces = jnp.take(flat_panel, cols_here, axis=0)
    pieces = jnp.where(alive_mask[:, None], pieces, jnp.zeros_like(pieces))
    pieces = pieces.reshape(span_slots, tile_side, width_k)
    tile_out = jnp.einsum("tab,tbk->tak", tiles_here, pieces, preferred_element_type=jnp.float32)
    return tile_out.reshape(span_slots, tile_side * width_k)


def place_rows(rows_slot, tile_out, row_tiles, tile_side, width_k):
    placed = jax.ops.segment_sum(tile_out, rows_slot, num_segments=row_tiles)
    return placed.reshape(row_tiles * tile_side, width_k)


def apply_operator(block, vertex_scale, tiles_here, rows_here, cols_here, count_here):
    tile_side = tiles_here.shape[-1]
    width_k = block.shape[1]
    slot_total = tiles_here.shape[0]
    scaled = (vertex_scale[:, None] * block).astype(jnp.bfloat16)
    gathered = lax.all_gather(scaled, "col", axis=0, tiled=True)
    flat_panel = gathered.reshape(gathered.shape[0] // tile_side, tile_side * width_k)
    row_tiles = lax.axis_size("row") * block.shape[0] // tile_side
    tile_out = tile_products(
        tiles_here, cols_here, count_here, flat_panel, slot_total, tile_side, width_k
    )
    partial_value = place_rows(rows_here, tile_out, row_tiles, tile_side, width_k)
    summed = lax.psum_scatter(
        partial_value.astype(jnp.bfloat16), "row", scatter_dimension=0, tiled=True
    ).astype(jnp.float32)
    return block - vertex_scale[:, None] * summed


def inner(left, right):
    return jnp.einsum("sk,sl->kl", left, right, precision=HIGH)


def residual_block(block, image, verts_all):
    gram = lax.psum(inner(block, image), ("row", "col")) / verts_all
    resid = image - jnp.dot(block, gram, precision=HIGH)
    colsq = lax.psum(jnp.sum(resid * resid, axis=0), ("row", "col"))
    return resid * lax.rsqrt(colsq / verts_all + 1e-06)


def local(
    start_block,
    vertex_scale,
    adj_tiles,
    tile_row,
    tile_col,
    live_count,
    rotation_first,
    rotation_second,
):
    width_k = start_block.shape[1]
    verts_all = start_block.shape[0] * lax.axis_size("row") * lax.axis_size("col")
    tiles_here = adj_tiles[0, 0]
    rows_here = tile_row[0, 0]
    cols_here = tile_col[0, 0]
    count_here = live_count[0, 0]

    def oper(block):
        return apply_operator(block, vertex_scale, tiles_here, rows_here, cols_here, count_here)

    image0 = oper(start_block)
    search0 = residual_block(start_block, image0, verts_all)
    simage0 = oper(search0)
    rot_x, rot_w = (rotation_first[:width_k], rotation_first[width_k:])
    block1 = jnp.dot(start_block, rot_x, precision=HIGH) + jnp.dot(search0, rot_w, precision=HIGH)
    image1 = jnp.dot(image0, rot_x, precision=HIGH) + jnp.dot(simage0, rot_w, precision=HIGH)
    prev1 = jnp.dot(search0, rot_w, precision=HIGH)
    pimage1 = jnp.dot(simage0, rot_w, precision=HIGH)
    search1 = residual_block(block1, image1, verts_all)
    simage1 = oper(search1)
    rot_qx = rotation_second[:width_k]
    rot_qw = rotation_second[width_k : 2 * width_k]
    rot_qp = rotation_second[2 * width_k :]
    final_block = (
        jnp.dot(block1, rot_qx, precision=HIGH)
        + jnp.dot(search1, rot_qw, precision=HIGH)
        + jnp.dot(prev1, rot_qp, precision=HIGH)
    )
    final_image = (
        jnp.dot(image1, rot_qx, precision=HIGH)
        + jnp.dot(simage1, rot_qw, precision=HIGH)
        + jnp.dot(pimage1, rot_qp, precision=HIGH)
    )
    return (final_block, final_image)


def solution(mesh):
    placed = (
        P(("row", "col"), None),
        P(("row", "col")),
        P("row", "col", None, None, None),
        P("row", "col", None),
        P("row", "col", None),
        P("row", "col"),
        P(),
        P(),
    )
    return jax.shard_map(
        local,
        mesh=mesh,
        in_specs=placed,
        out_specs=(P(("row", "col"), None), P(("row", "col"), None)),
        check_vma=False,
    )
```

profile of v0, /device:TPU:2, one launch (start us, length us, event | category | flops | bytes accessed | tf_op | source)
XLA Modules:
  0.0 1100.4 jit_solution(16218495195349804594)
XLA Ops:
  11.7 39.2 %all-gather.4.cloned.1.call-done = bf16[4096,128]{0,1:T(8,128)(2,1)} async-done(((bf16[256,128]{0,1:T(8,128)(2,1)}), bf16[4096,128]{0,1:T(8,128)(2,1)}) %all-gather.4.cloned.1.call-update) | async-done | bytes 1048592 | tf_op jit(solution)/shard_map/all_gather | solution.py:28
  54.8 3.2 gather_fusion
  60.5 3.6 convolution_bitcast_fusion.2
  64.0 5.6 copy.21
  69.6 10.6 scatter_custom_fusion
  85.6 76.8 %reduce-scatter.4.cloned.1.call-done = bf16[256,128]{0,1:T(8,128)(2,1)} async-done(((bf16[4096,128]{0,1:T(8,128)(2,1)}), bf16[256,128]{0,1:T(8,128)(2,1)}) %reduce-scatter.4.cloned.1.call-update) | async-done | bytes 65552 | tf_op jit(solution)/shard_map/reduce_scatter | solution.py:35
  164.3 241.9 %all-reduce.3.cloned.1.call-done = f32[128,128]{0,1:T(8,128)} async-done(((f32[128,128]{0,1:T(8,128)}), f32[128,128]{0,1:T(8,128)}) %all-reduce.3.cloned.1.call-update) | async-done | bytes 65552 | tf_op jit(solution)/shard_map/psum | solution.py:46
  407.4 74.2 %psum.29 = f32[128]{0:T(128)S(1)} all-reduce(f32[128]{0:T(128)S(1)} %get-tuple-element.3), channel_id=1, replica_groups=mesh['row'=16,'col'=16] {'row','col'}, use_global_device_ids=true, to_apply=%region_4.6 | all-reduce | flops 128 | bytes 1024 | tf_op jit(solution)/shard_map/psum | solution.py:48
  483.1 33.3 %all-gather.6.cloned.1.call-done = bf16[4096,128]{0,1:T(8,128)(2,1)} async-done(((bf16[256,128]{0,1:T(8,128)(2,1)}), bf16[4096,128]{0,1:T(8,128)(2,1)}) %all-gather.6.cloned.1.call-update) | async-done | bytes 1048592 | tf_op jit(solution)/shard_map/all_gather | solution.py:28
  520.2 3.2 gather_fusion.1
  525.9 3.6 convolution_bitcast_fusion.1
  529.5 5.6 copy.26
  535.1 10.6 scatter_custom_fusion.1
  548.7 2.3 copy.27
  552.1 75.8 %reduce-scatter.6.cloned.1.call-done = bf16[256,128]{0,1:T(8,128)(2,1)} async-done(((bf16[4096,128]{0,1:T(8,128)(2,1)}), bf16[256,128]{0,1:T(8,128)(2,1)}) %reduce-scatter.6.cloned.1.call-update) | async-done | bytes 65552 | tf_op jit(solution)/shard_map/reduce_scatter | solution.py:35
  631.2 238.6 %all-reduce.5.cloned.1.call-done = f32[128,128]{0,1:T(8,128)} async-done(((f32[128,128]{0,1:T(8,128)}), f32[128,128]{0,1:T(8,128)}) %all-reduce.5.cloned.1.call-update) | async-done | bytes 65552 | tf_op jit(solution)/shard_map/psum | solution.py:46
  871.0 74.2 %psum.31 = f32[128]{0:T(128)S(1)} all-reduce(f32[128]{0:T(128)S(1)} %get-tuple-element.5), channel_id=1, replica_groups=mesh['row'=16,'col'=16] {'row','col'}, use_global_device_ids=true, to_apply=%region_9.11 | all-reduce | flops 128 | bytes 1024 | tf_op jit(solution)/shard_map/psum | solution.py:48
  946.0 33.5 %all-gather.8.cloned.1.call-done = bf16[4096,128]{0,1:T(8,128)(2,1)} async-done(((bf16[256,128]{0,1:T(8,128)(2,1)}), bf16[4096,128]{0,1:T(8,128)(2,1)}) %all-gather.8.cloned.1.call-update) | async-done | bytes 1048592 | tf_op jit(solution)/shard_map/all_gather | solution.py:28
  983.3 3.2 gather_fusion.2
  989.0 3.6 convolution_bitcast_fusion
  992.6 5.6 copy.33
  998.2 10.6 scatter_custom_fusion.2
  1011.8 2.3 copy.34
  1016.2 74.7 %reduce-scatter.8.cloned.1.call-done = bf16[256,128]{0,1:T(8,128)(2,1)} async-done(((bf16[4096,128]{0,1:T(8,128)(2,1)}), bf16[256,128]{0,1:T(8,128)(2,1)}) %reduce-scatter.8.cloned.1.call-update) | async-done | bytes 65552 | tf_op jit(solution)/shard_map/reduce_scatter | solution.py:35
  (87 shorter events, 49.0 us)
Async XLA Ops:
  7.2 53.3 %copy-start = (bf16[1,1,64,128,128]{4,3,2,1,0:T(8,128)(2,1)S(1)}, bf16[1,1,64,128,128]{4,3,2,1,0:T(8,128)(2,1)}, u32[]{:S(2)}) copy-start(bf16[1,1,64,128,128]{4,3,2,1,0:T(8,128)(2,1)} %param.12) | copy-start | bytes 6291460
  7.2 43.8 %all-gather.4.cloned.1.call-start = ((), (), s32[]{:S(2)}) async-start(), calls=%async_computation.3 | async-start | bytes 1114112 | tf_op jit(solution)/shard_map/all_gather | solution.py:28
  9.7 152.7 %reduce-scatter.4.cloned.1.call-start = ((), (), s32[]{:S(2)}) async-start(), calls=%async_computation.4 | async-start | bytes 1114112 | tf_op jit(solution)/shard_map/reduce_scatter | solution.py:35
  83.3 79.2 %copy-start.1 = (f32[256,128]{1,0:T(8,128)S(1)}, f32[256,128]{1,0:T(8,128)}, u32[]{:S(2)}) copy-start(f32[256,128]{1,0:T(8,128)} %param.10) | copy-start | bytes 393220
  83.3 79.2 %copy-start.11 = (f32[256]{0:T(256)S(1)}, f32[256]{0:T(256)}, u32[]{:S(2)}) copy-start(f32[256]{0:T(256)} %param.11) | copy-start | bytes 3076
  85.6 320.6 %all-reduce.3.cloned.1.call-start = ((), (), s32[]{:S(2)}) async-start(), calls=%async_computation.5 | async-start | bytes 131072 | tf_op jit(solution)/shard_map/psum | solution.py:46
  164.2 352.2 %all-gather.6.cloned.1.call-start = ((), (), s32[]{:S(2)}) async-start(), calls=%async_computation.6 | async-start | bytes 1114112 | tf_op jit(solution)/shard_map/all_gather | solution.py:28
  481.6 0.5 copy-start.12
  482.9 145.0 %reduce-scatter.6.cloned.1.call-start = ((), (), s32[]{:S(2)}) async-start(), calls=%async_computation.7 | async-start | bytes 1114112 | tf_op jit(solution)/shard_map/reduce_scatter | solution.py:35
  548.7 2.6 copy-start.10
  548.7 2.6 copy-start.13
  548.7 81.2 %copy-start.9 = (bf16[256,128]{0,1:T(8,128)(2,1)S(1)}, bf16[256,128]{0,1:T(8,128)(2,1)}, u32[]{:S(2)}) copy-start(bf16[256,128]{0,1:T(8,128)(2,1)} %reduce-scatter.4.cloned.1.call-done) | copy-start | bytes 196612
  551.0 318.8 %all-reduce.5.cloned.1.call-start = ((), (), s32[]{:S(2)}) async-start(), calls=%async_computation.8 | async-start | bytes 131072 | tf_op jit(solution)/shard_map/psum | solution.py:46
  551.8 427.7 %copy-start.4 = (f32[256,128]{1,0:T(8,128)}, f32[256,128]{1,0:T(8,128)S(1)}, u32[]{:S(2)}) copy-start(f32[256,128]{1,0:T(8,128)S(1)} %fusion.29) | copy-start | bytes 393220
  552.1 427.4 %copy-start.2 = (f32[256,128]{1,0:T(8,128)}, f32[256,128]{1,0:T(8,128)S(1)}, u32[]{:S(2)}) copy-start(f32[256,128]{1,0:T(8,128)S(1)} %convolution_add_fusion.5) | copy-start | bytes 393220
  629.2 0.6 copy-start.6
  631.2 348.3 %all-gather.8.cloned.1.call-start = ((), (), s32[]{:S(2)}) async-start(), calls=%async_computation.9 | async-start | bytes 1114112 | tf_op jit(solution)/shard_map/all_gather | solution.py:28
  945.9 145.0 %reduce-scatter.8.cloned.1.call-start = ((), (), s32[]{:S(2)}) async-start(), calls=%async_computation.10 | async-start | bytes 1114112 | tf_op jit(solution)/shard_map/reduce_scatter | solution.py:35
  1011.8 2.3 copy-start.3
  1011.8 2.4 copy-start.8
  1011.8 3.5 copy-start.5
  1014.1 78.1 %copy-start.7 = (f32[256,128]{1,0:T(8,128)S(1)}, f32[256,128]{1,0:T(8,128)}, u32[]{:S(2)}) copy-start(f32[256,128]{1,0:T(8,128)} %copy-done.6) | copy-start | bytes 393220
Sparse Core Ops, SparseCore 0:
  10.3 40.5 all-gather.3
  85.7 76.6 reduce-scatter.3
  169.4 236.6 all-reduce.2
  483.0 33.3 all-gather.5
  551.2 76.6 reduce-scatter.5
  633.3 236.4 all-reduce.4
  946.1 33.3 all-gather.7
  1014.2 76.6 reduce-scatter.7
where the time goes:
time: 1110 us; the launch traced here: 1100 us
  waiting for transfers between devices  814 us (73%)
  blocking collectives  148 us (13%)
  local copies, waits for them, and re-layouts  52.7 us (5%)
  other arithmetic  46.7 us (4%)
  matrix products  22.4 us (2%)
  between operations  15.4 us (1%)
    psum x2, waiting for transfers between devices, residual_block(): gram = lax.psum(inner(block, image), ('row', 'col')) / verts_all  480 us
    reduce_scatter x3, waiting for transfers between devices, apply_operator(): lax.psum_scatter(partial_value.astype(jnp.bfloat16), 'row', scatter_dimen...  227 us
    psum x2, blocking collectives, residual_block(): colsq = lax.psum(jnp.sum(resid * resid, axis=0), ('row', 'col'))  148 us
    all_gather x3, waiting for transfers between devices, apply_operator(): gathered = lax.all_gather(scaled, 'col', axis=0, tiled=True)  106 us
    scatter-add x3, other arithmetic, place_rows(): placed = jax.ops.segment_sum(tile_out, rows_slot, num_segments=row_tiles)  31.9 us
  transfers between devices with their start and end apart: 8, of which 8 were waited for; matrix products, arithmetic and copies ran while one was open for 0% of the time, Pallas kernels for 0%

commit v1 on v0

--- a/solution.py
+++ b/solution.py
@@ -43,7 +43,7 @@
 
 
 def residual_block(block, image, verts_all):
-    gram = lax.psum(inner(block, image), ("row", "col")) / verts_all
+    gram = lax.psum(lax.psum(inner(block, image), "row"), "col") / verts_all
     resid = image - jnp.dot(block, gram, precision=HIGH)
     colsq = lax.psum(jnp.sum(resid * resid, axis=0), ("row", "col"))
     return resid * lax.rsqrt(colsq / verts_all + 1e-06)

time: 1110 us -> 1020 us (0.919)
  waiting for transfers between devices: 814 us -> 722 us
    psum x2 -> x4, waiting for transfers between devices: 480 us -> 385 us  [residual_block(): gram = lax.psum(lax.psum(inner(block, image), 'row'), 'col') / verts_all]
  transfers between devices with their start and end apart: 8 -> 10, of which waited for: 8 -> 10; matrix products, arithmetic and copies ran while one was open for 0% -> 0% of each run, Pallas kernels for 0% -> 0%
where the time goes in v1:
time: 1020 us; the launch traced here: 1010 us
  waiting for transfers between devices  722 us (71%)
  blocking collectives  151 us (15%)
  local copies, waits for them, and re-layouts  52.7 us (5%)
  other arithmetic  46.7 us (5%)
  matrix products  22.4 us (2%)
  between operations  15.5 us (2%)
    psum x4, waiting for transfers between devices, residual_block(): gram = lax.psum(lax.psum(inner(block, image), 'row'), 'col') / verts_all  385 us
    reduce_scatter x3, waiting for transfers between devices, apply_operator(): lax.psum_scatter(partial_value.astype(jnp.bfloat16), 'row', scatter_dimen...  227 us
    psum x2, blocking collectives, residual_block(): colsq = lax.psum(jnp.sum(resid * resid, axis=0), ('row', 'col'))  151 us
    all_gather x3, waiting for transfers between devices, apply_operator(): gathered = lax.all_gather(scaled, 'col', axis=0, tiled=True)  110 us
    scatter-add x3, other arithmetic, place_rows(): placed = jax.ops.segment_sum(tile_out, rows_slot, num_segments=row_tiles)  31.9 us
  transfers between devices with their start and end apart: 10, of which 10 were waited for; matrix products, arithmetic and copies ran while one was open for 0% of the time, Pallas kernels for 0%

profile of v1, /device:TPU:2, one launch (start us, length us, event | category | flops | bytes accessed | tf_op | source)
XLA Modules:
  0.0 1010.6 jit_solution(13561271771964962593)
XLA Ops:
  11.7 39.2 %all-gather.4.cloned.1.call-done = bf16[4096,128]{0,1:T(8,128)(2,1)} async-done(((bf16[256,128]{0,1:T(8,128)(2,1)}), bf16[4096,128]{0,1:T(8,128)(2,1)}) %all-gather.4.cloned.1.call-update) | async-done | bytes 1048592 | tf_op jit(solution)/shard_map/all_gather | solution.py:28
  54.8 3.2 gather_fusion
  60.5 3.6 convolution_bitcast_fusion.2
  64.0 5.6 copy.21
  69.6 10.6 %scatter_custom_fusion = f32[32,16384]{1,0:T(8,128)} fusion(s32[64]{0:T(128)} %bitcast.66, f32[8,8,128,128]{3,2,1,0:T(8,128)} %bitcast.61, f32[]{:T(128)} %constant.4.clone.1), kind=kCustom, calls=%fused_computation.12 | custom fusion | flops 1048576 | bytes 6291968 | tf_op jit(solution)/shard_map/scatter-add | solution.py:19
  85.6 76.8 %reduce-scatter.4.cloned.1.call-done = bf16[256,128]{0,1:T(8,128)(2,1)} async-done(((bf16[4096,128]{0,1:T(8,128)(2,1)}), bf16[256,128]{0,1:T(8,128)(2,1)}) %reduce-scatter.4.cloned.1.call-update) | async-done | bytes 65552 | tf_op jit(solution)/shard_map/reduce_scatter | solution.py:35
  164.3 92.8 %all-reduce.5.cloned.1.call-done = f32[128,128]{0,1:T(8,128)} async-done(((f32[128,128]{0,1:T(8,128)}), f32[128,128]{0,1:T(8,128)}) %all-reduce.5.cloned.1.call-update) | async-done | bytes 65552 | tf_op jit(solution)/shard_map/psum | solution.py:46
  257.1 100.6 %all-reduce.7.cloned.1.call-done = f32[128,128]{0,1:T(8,128)} async-done(((f32[128,128]{0,1:T(8,128)}), f32[128,128]{0,1:T(8,128)}) %all-reduce.7.cloned.1.call-update) | async-done | bytes 65552 | tf_op jit(solution)/shard_map/psum | solution.py:46
  359.0 75.3 %psum.44 = f32[128]{0:T(128)S(1)} all-reduce(f32[128]{0:T(128)S(1)} %get-tuple-element.3), channel_id=1, replica_groups=mesh['row'=16,'col'=16] {'row','col'}, use_global_device_ids=true, to_apply=%region_5.7 | all-reduce | flops 128 | bytes 1024 | tf_op jit(solution)/shard_map/psum | solution.py:48
  435.8 35.1 %all-gather.6.cloned.1.call-done = bf16[4096,128]{0,1:T(8,128)(2,1)} async-done(((bf16[256,128]{0,1:T(8,128)(2,1)}), bf16[4096,128]{0,1:T(8,128)(2,1)}) %all-gather.6.cloned.1.call-update) | async-done | bytes 1048592 | tf_op jit(solution)/shard_map/all_gather | solution.py:28
  474.7 3.2 gather_fusion.1
  480.3 3.6 convolution_bitcast_fusion.1
  483.9 5.6 copy.26
  489.5 10.6 %scatter_custom_fusion.1 = f32[32,16384]{1,0:T(8,128)} fusion(s32[64]{0:T(128)} %bitcast.67, f32[8,8,128,128]{3,2,1,0:T(8,128)} %bitcast.62, f32[]{:T(128)} %constant.4.clone.1), kind=kCustom, calls=%fused_computation.9 | custom fusion | flops 1048576 | bytes 6291968 | tf_op jit(solution)/shard_map/scatter-add | solution.py:19
  506.5 75.8 %reduce-scatter.6.cloned.1.call-done = bf16[256,128]{0,1:T(8,128)(2,1)} async-done(((bf16[4096,128]{0,1:T(8,128)(2,1)}), bf16[256,128]{0,1:T(8,128)(2,1)}) %reduce-scatter.6.cloned.1.call-update) | async-done | bytes 65552 | tf_op jit(solution)/shard_map/reduce_scatter | solution.py:35
  585.6 90.5 %all-reduce.9.cloned.1.call-done = f32[128,128]{0,1:T(8,128)} async-done(((f32[128,128]{0,1:T(8,128)}), f32[128,128]{0,1:T(8,128)}) %all-reduce.9.cloned.1.call-update) | async-done | bytes 65552 | tf_op jit(solution)/shard_map/psum | solution.py:46
  676.2 100.9 %all-reduce.11.cloned.1.call-done = f32[128,128]{0,1:T(8,128)} async-done(((f32[128,128]{0,1:T(8,128)}), f32[128,128]{0,1:T(8,128)}) %all-reduce.11.cloned.1.call-update) | async-done | bytes 65552 | tf_op jit(solution)/shard_map/psum | solution.py:46
  778.3 75.3 %psum.47 = f32[128]{0:T(128)S(1)} all-reduce(f32[128]{0:T(128)S(1)} %get-tuple-element.5), channel_id=1, replica_groups=mesh['row'=16,'col'=16] {'row','col'}, use_global_device_ids=true, to_apply=%region_11.13 | all-reduce | flops 128 | bytes 1024 | tf_op jit(solution)/shard_map/psum | solution.py:48
  854.4 35.2 %all-gather.8.cloned.1.call-done = bf16[4096,128]{0,1:T(8,128)(2,1)} async-done(((bf16[256,128]{0,1:T(8,128)(2,1)}), bf16[4096,128]{0,1:T(8,128)(2,1)}) %all-gather.8.cloned.1.call-update) | async-done | bytes 1048592 | tf_op jit(solution)/shard_map/all_gather | solution.py:28
  893.5 3.2 gather_fusion.2
  899.1 3.6 convolution_bitcast_fusion
  902.7 5.6 copy.33
  908.3 10.6 %scatter_custom_fusion.2 = f32[32,16384]{1,0:T(8,128)} fusion(s32[64]{0:T(128)} %bitcast.68, f32[8,8,128,128]{3,2,1,0:T(8,128)} %bitcast.60, f32[]{:T(128)} %constant.4.clone.1), kind=kCustom, calls=%fused_computation.6 | custom fusion | flops 1048576 | bytes 6291968 | tf_op jit(solution)/shard_map/scatter-add | solution.py:19
  926.4 74.8 %reduce-scatter.8.cloned.1.call-done = bf16[256,128]{0,1:T(8,128)(2,1)} async-done(((bf16[4096,128]{0,1:T(8,128)(2,1)}), bf16[256,128]{0,1:T(8,128)(2,1)}) %reduce-scatter.8.cloned.1.call-update) | async-done | bytes 65552 | tf_op jit(solution)/shard_map/reduce_scatter | solution.py:35
  (93 shorter events, 53.7 us)
Async XLA Ops:
  7.2 53.3 %copy-start = (bf16[1,1,64,128,128]{4,3,2,1,0:T(8,128)(2,1)S(1)}, bf16[1,1,64,128,128]{4,3,2,1,0:T(8,128)(2,1)}, u32[]{:S(2)}) copy-start(bf16[1,1,64,128,128]{4,3,2,1,0:T(8,128)(2,1)} %param.12) | copy-start | bytes 6291460
  7.2 43.8 %all-gather.4.cloned.1.call-start = ((), (), s32[]{:S(2)}) async-start(), calls=%async_computation.3 | async-start | bytes 1114112 | tf_op jit(solution)/shard_map/all_gather | solution.py:28
  9.7 152.7 %reduce-scatter.4.cloned.1.call-start = ((), (), s32[]{:S(2)}) async-start(), calls=%async_computation.4 | async-start | bytes 1114112 | tf_op jit(solution)/shard_map/reduce_scatter | solution.py:35
  83.3 79.2 %copy-start.1 = (f32[256,128]{1,0:T(8,128)S(1)}, f32[256,128]{1,0:T(8,128)}, u32[]{:S(2)}) copy-start(f32[256,128]{1,0:T(8,128)} %param.10) | copy-start | bytes 393220
  83.3 79.2 %copy-start.11 = (f32[256]{0:T(256)S(1)}, f32[256]{0:T(256)}, u32[]{:S(2)}) copy-start(f32[256]{0:T(256)} %param.11) | copy-start | bytes 3076
  85.6 171.5 %all-reduce.5.cloned.1.call-start = ((), (), s32[]{:S(2)}) async-start(), calls=%async_computation.5 | async-start | bytes 131072 | tf_op jit(solution)/shard_map/psum | solution.py:46
  164.2 193.5 %all-reduce.7.cloned.1.call-start = ((), (), s32[]{:S(2)}) async-start(), calls=%async_computation.6 | async-start | bytes 131072 | tf_op jit(solution)/shard_map/psum | solution.py:46
  257.1 213.8 %all-gather.6.cloned.1.call-start = ((), (), s32[]{:S(2)}) async-start(), calls=%async_computation.7 | async-start | bytes 1114112 | tf_op jit(solution)/shard_map/all_gather | solution.py:28
  434.3 0.5 copy-start.12
  435.6 146.7 %reduce-scatter.6.cloned.1.call-start = ((), (), s32[]{:S(2)}) async-start(), calls=%async_computation.8 | async-start | bytes 1114112 | tf_op jit(solution)/shard_map/reduce_scatter | solution.py:35
  503.1 2.6 copy-start.10
  503.2 2.6 copy-start.13
  503.2 81.2 %copy-start.9 = (bf16[256,128]{0,1:T(8,128)(2,1)S(1)}, bf16[256,128]{0,1:T(8,128)(2,1)}, u32[]{:S(2)}) copy-start(bf16[256,128]{0,1:T(8,128)(2,1)} %reduce-scatter.4.cloned.1.call-done) | copy-start | bytes 196612
  505.5 170.7 %all-reduce.9.cloned.1.call-start = ((), (), s32[]{:S(2)}) async-start(), calls=%async_computation.9 | async-start | bytes 131072 | tf_op jit(solution)/shard_map/psum | solution.py:46
  506.2 383.4 %copy-start.4 = (f32[256,128]{1,0:T(8,128)}, f32[256,128]{1,0:T(8,128)S(1)}, u32[]{:S(2)}) copy-start(f32[256,128]{1,0:T(8,128)S(1)} %fusion.29) | copy-start | bytes 393220
  506.5 383.2 %copy-start.2 = (f32[256,128]{1,0:T(8,128)}, f32[256,128]{1,0:T(8,128)S(1)}, u32[]{:S(2)}) copy-start(f32[256,128]{1,0:T(8,128)S(1)} %convolution_add_fusion.5) | copy-start | bytes 393220
  583.6 0.6 copy-start.6
  585.6 191.5 %all-reduce.11.cloned.1.call-start = ((), (), s32[]{:S(2)}) async-start(), calls=%async_computation.10 | async-start | bytes 131072 | tf_op jit(solution)/shard_map/psum | solution.py:46
  676.2 213.5 %all-gather.8.cloned.1.call-start = ((), (), s32[]{:S(2)}) async-start(), calls=%async_computation.11 | async-start | bytes 1114112 | tf_op jit(solution)/shard_map/all_gather | solution.py:28
  854.4 146.8 %reduce-scatter.8.cloned.1.call-start = ((), (), s32[]{:S(2)}) async-start(), calls=%async_computation.12 | async-start | bytes 1114112 | tf_op jit(solution)/shard_map/reduce_scatter | solution.py:35
  921.9 2.3 copy-start.3
  921.9 2.4 copy-start.8
  922.0 3.5 copy-start.5
  924.3 78.2 %copy-start.7 = (f32[256,128]{1,0:T(8,128)S(1)}, f32[256,128]{1,0:T(8,128)}, u32[]{:S(2)}) copy-start(f32[256,128]{1,0:T(8,128)} %copy-done.6) | copy-start | bytes 393220
Sparse Core Ops, SparseCore 0:
  10.3 40.5 all-gather.3
  85.7 76.6 reduce-scatter.3
  166.5 90.4 all-reduce.4
  259.2 98.4 all-reduce.6
  435.7 35.1 all-gather.5
  505.6 76.6 reduce-scatter.5
  585.7 90.4 all-reduce.8
  678.6 98.4 all-reduce.10
  854.5 35.1 all-gather.7
  924.4 76.6 reduce-scatter.7
